TPU v7x, 256 devices: a whole 4x4x8 slice. The times are simulated.
256 devices in a mesh: band: 8 (over y, core), tm: 32 (over x, z).
Axes of the slice: x: 4, y: 4, z: 8, core: 2. Of those that a mesh axis runs over, the one named last changes fastest.
Arguments:
- tod: bfloat16 [8, 64, 262144], P('band', None, 'tm'), may hold values from -6 to 6
- filter_taps: bfloat16 [8, 64, 2049], P('band'), may hold values from -0.125 to 0.125
- det_weights: float32 [8, 64], P('band'), may hold values from -0.75 to 0.75
- owner: int32 [8, 2048, 1], P('band', 'tm'), may hold values from 0 to 31; in each aligned block of 64 rows (0 to 63, 64 to 127, ..., all dimensions but the last counted through in order) at most 8 rows name the same one
- tile_row: int32 [8, 2048], P('band', 'tm'), may hold values from 0 to 127
- block_counts: int32 [8, 32], P('band', 'tm'), may hold values from 32 to 64, as said below
- beam_rows: float32 [8, 2, 33], P('band'), may hold values from -1 to 1
- beam_cols: float32 [8, 2, 33], P('band'), may hold values from -1 to 1
- mixing: float32 [4, 8, 2], P(None, 'band'), may hold values from -1.5 to 1.5
Outputs:
- components: float32 [4, 32, 128, 128], P(None, 'tm', 'band')
Inputs may be any that keep to these rules, and one draw needn't show every extreme that they name: The owner of each scan block; among the 64 scan blocks of one time shard of one band at most 8 share an owner, and in every draw some time shard sends exactly 8 to one owner. A time shard keeps its first block_counts scan blocks, the rest carry nothing; the largest value is reached in every draw.
All inputs are finite; a program needn't handle non-finite values.
Results may differ from a plain program's by a relative error of at most 0.0003.
Values may be sent and summed in bfloat16 or wider, within the bound.
A program may use at most 128 MiB of HBM per device.

v0:
```python
import math

import jax
import jax.numpy as jnp
from jax import lax
from jax.sharding import PartitionSpec as P

PIX = 128
TROWS = 128


def with_halo(array, sides, width):
    for axis, dim in sides:
        count, length = (lax.axis_size(axis), array.shape[dim])
        up = [(i, (i + 1) % count) for i in range(count - 1)]
        down = [(j, i) for i, j in up]
        last = lax.slice_in_dim(array, length - width, length, axis=dim)
        leading = lax.slice_in_dim(array, 0, width, axis=dim)
        before = lax.ppermute(last, axis, up)
        after = lax.ppermute(leading, axis, down)
        array = jnp.concatenate([before, array, after], axis=dim)
    return array


def toeplitz_rows(tap_row, seg_len):
    taps = tap_row.shape[0]
    width = seg_len + taps - 1
    padded_taps = jnp.concatenate([tap_row, jnp.zeros((seg_len,), tap_row.dtype)])
    tiled = jnp.tile(padded_taps, seg_len)[: seg_len * width]
    return tiled.reshape(seg_len, width)


def filter_group(group_args):
    padded_group, tap_group = group_args
    half_len = (tap_group.shape[1] - 1) // 2
    seg_len = math.gcd(half_len, 128)
    reach_pieces = 2 * half_len // seg_len
    group_size = padded_group.shape[0]
    segments = (padded_group.shape[1] - 2 * half_len) // seg_len
    pieces = padded_group.reshape(group_size, segments + reach_pieces, seg_len)
    windows = jnp.concatenate(
        [pieces[:, shift : shift + segments] for shift in range(reach_pieces + 1)], axis=2
    )
    tables = jax.vmap(lambda tap_row: toeplitz_rows(tap_row, seg_len))(tap_group)
    product = lax.dot_general(
        windows, tables, (((2,), (2,)), ((0,), (0,))), preferred_element_type=jnp.float32
    )
    return product.reshape(group_size, segments * seg_len)


def band_matrix(profiles, out_size, in_size, offset):
    width = profiles.shape[1]
    spread = lax.iota(jnp.int32, in_size)[None, :] - lax.iota(jnp.int32, out_size)[:, None] + offset
    picks = (spread[None, :, :] == lax.iota(jnp.int32, width)[:, None, None]).astype(jnp.float32)
    return jnp.einsum("ka,arq->krq", profiles, picks, precision=lax.Precision.HIGHEST)


def on_device(
    tod, filter_taps, det_weights, owner, tile_row, block_counts, beam_rows, beam_cols, mixing
):
    tap_rows = filter_taps[0]
    half_len = (tap_rows.shape[1] - 1) // 2
    detectors = tod.shape[1]
    samples = tod.shape[2]
    group_size = math.gcd(detectors, 16)
    padded = with_halo(tod, (("tm", 2),), half_len)[0]
    padded = padded.reshape(detectors // group_size, group_size, samples + 2 * half_len)
    grouped_taps = tap_rows.reshape(detectors // group_size, group_size, tap_rows.shape[1])
    filtered = lax.map(filter_group, (padded, grouped_taps))
    filtered = filtered.reshape(detectors, samples)
    weighted = jnp.dot(
        det_weights[0],
        filtered,
        precision=lax.Precision.HIGHEST,
        preferred_element_type=jnp.float32,
    )
    blocks_here = samples // PIX
    block_vals = weighted.reshape(blocks_here, PIX)
    valid_mask = (lax.iota(jnp.int32, blocks_here) < block_counts[0, 0]).astype(jnp.float32)
    block_vals = block_vals * valid_mask[:, None]
    owners = owner[0, :, 0]
    pixel_rows = tile_row[0]
    target = owners * TROWS + pixel_rows
    row_ids = lax.iota(jnp.int32, TROWS * lax.axis_size("tm"))
    hits = (row_ids[:, None] == target[None, :]).astype(jnp.float32)
    tile = lax.psum_scatter(
        jnp.dot(
            hits, block_vals, precision=lax.Precision.HIGHEST, preferred_element_type=jnp.float32
        ),
        "tm",
        scatter_dimension=0,
        tiled=True,
    )
    beam_reach = (beam_rows.shape[2] - 1) // 2
    extended = with_halo(tile, (("tm", 0),), beam_reach)
    row_mats = band_matrix(beam_rows[0], TROWS, TROWS + 2 * beam_reach, 0)
    col_mats = band_matrix(beam_cols[0], PIX, PIX, beam_reach)
    rowed = jnp.einsum("krq,qc->krc", row_mats, extended, precision=lax.Precision.HIGHEST)
    beamed = jnp.einsum("krc,kxc->krx", rowed, col_mats, precision=lax.Precision.HIGHEST)
    local_mix = jnp.einsum("ck,krx->crx", mixing[:, 0, :], beamed, precision=lax.Precision.HIGHEST)
    total = lax.psum(local_mix, "band")
    share = TROWS // lax.axis_size("band")
    mine = lax.dynamic_slice_in_dim(total, lax.axis_index("band") * share, share, 1)
    return mine[:, None]


def solution(mesh):
    placed = (
        P("band", None, "tm"),
        P("band", None, None),
        P("band", None),
        P("band", "tm", None),
        P("band", "tm"),
        P("band", "tm"),
        P("band", None, None),
        P("band", None, None),
        P(None, "band", None),
    )
    return jax.shard_map(
        on_device,
        mesh=mesh,
        in_specs=placed,
        out_specs=P(None, "tm", "band", None),
        check_vma=False,
    )
```

profile of v0, /device:TPU:1, one launch (start us, length us, event | category | flops | bytes accessed | tf_op | source)
XLA Modules:
  0.0 553.0 jit_solution(13998060407208379251)
XLA Ops:
  7.5 4.4 collective-permute-start
  19.6 221.9 %while.10 = (s32[]{:T(128)}, f32[4,16,8192]{2,1,0:T(8,128)}, bf16[4,16,10240]{2,1,0:T(8,128)(2,1)S(1)}, bf16[4,16,2049]{2,1,0:T(8,128)(2,1)}, s32[]{:T(128)}, /*index=5*/bf16[]{:T(256)}) while((s32[]{:T(128)}, f32[4,16,8192]{2,1,0:T(8,128)}, bf16[4,16,10240]{2,1,0:T(8,128)(2,1)S(1)}, bf16[4,16,2049]{2,1,0:T(8,128)(2,1)}, s32[]{:T(128)}, ...), condition=%wide.region_1.2_spmd, body=%wide.region_0.1_spmd.sunk | while | flops 570425344 | bytes 106779400 | solution.py:69
  24.6 4.3 tile.11
  28.9 21.2 %tile.12 = bf16[16,278656]{1,0:T(8,128)(2,1)} reshape(bf16[16,128,2177]{2,1,0:T(8,128)(2,1)} %tile.11) | data formatting | bytes 17833984 | tf_op jit(solution)/shard_map/while/body/eval_jaxpr/vmap()/tile | solution.py:29
  50.1 7.4 %slice.146 = bf16[16,278528]{1,0:T(8,128)(2,1)} slice(bf16[16,278656]{1,0:T(8,128)(2,1)} %tile.12), slice={[0:16], [0:278528]} | slice | bytes 17825792 | tf_op jit(solution)/shard_map/while/body/eval_jaxpr/vmap()/slice | solution.py:29
  57.5 8.5 %copy.37 = bf16[2,8,128,2176]{3,2,1,0:T(8,128)(2,1)} copy(bf16[2,8,128,2176]{3,1,2,0:T(8,128)(2,1)} %bitcast.89) | data formatting | bytes 17825792 | tf_op jit(solution)/shard_map/while
  66.0 8.1 %fusion.39 = f32[16,64,128]{2,1,0:T(8,128)S(1)} fusion(bf16[16,64,2176]{2,1,0:T(8,128)(2,1)} %copy-done.1, bf16[16,128,2176]{2,1,0:T(8,128)(2,1)} %bitcast.90), kind=kOutput, calls=%fused_computation.61.clone.1 | convolution fusion | flops 570425344 | bytes 13893632 | tf_op jit(solution)/shard_map/while/body/eval_jaxpr/dot_general | solution.py:45
  80.1 4.3 tile.11
  84.3 21.2 %tile.12 = bf16[16,278656]{1,0:T(8,128)(2,1)} reshape(bf16[16,128,2177]{2,1,0:T(8,128)(2,1)} %tile.11) | data formatting | bytes 17833984 | tf_op jit(solution)/shard_map/while/body/eval_jaxpr/vmap()/tile | solution.py:29
  105.5 7.4 %slice.146 = bf16[16,278528]{1,0:T(8,128)(2,1)} slice(bf16[16,278656]{1,0:T(8,128)(2,1)} %tile.12), slice={[0:16], [0:278528]} | slice | bytes 17825792 | tf_op jit(solution)/shard_map/while/body/eval_jaxpr/vmap()/slice | solution.py:29
  113.0 8.5 %copy.37 = bf16[2,8,128,2176]{3,2,1,0:T(8,128)(2,1)} copy(bf16[2,8,128,2176]{3,1,2,0:T(8,128)(2,1)} %bitcast.89) | data formatting | bytes 17825792 | tf_op jit(solution)/shard_map/while
  121.4 8.2 %fusion.39 = f32[16,64,128]{2,1,0:T(8,128)S(1)} fusion(bf16[16,64,2176]{2,1,0:T(8,128)(2,1)} %copy-done.1, bf16[16,128,2176]{2,1,0:T(8,128)(2,1)} %bitcast.90), kind=kOutput, calls=%fused_computation.61.clone.1 | convolution fusion | flops 570425344 | bytes 13893632 | tf_op jit(solution)/shard_map/while/body/eval_jaxpr/dot_general | solution.py:45
  135.6 4.3 tile.11
  139.8 21.2 %tile.12 = bf16[16,278656]{1,0:T(8,128)(2,1)} reshape(bf16[16,128,2177]{2,1,0:T(8,128)(2,1)} %tile.11) | data formatting | bytes 17833984 | tf_op jit(solution)/shard_map/while/body/eval_jaxpr/vmap()/tile | solution.py:29
  161.0 7.4 %slice.146 = bf16[16,278528]{1,0:T(8,128)(2,1)} slice(bf16[16,278656]{1,0:T(8,128)(2,1)} %tile.12), slice={[0:16], [0:278528]} | slice | bytes 17825792 | tf_op jit(solution)/shard_map/while/body/eval_jaxpr/vmap()/slice | solution.py:29
  168.4 8.5 %copy.37 = bf16[2,8,128,2176]{3,2,1,0:T(8,128)(2,1)} copy(bf16[2,8,128,2176]{3,1,2,0:T(8,128)(2,1)} %bitcast.89) | data formatting | bytes 17825792 | tf_op jit(solution)/shard_map/while
  176.9 8.2 %fusion.39 = f32[16,64,128]{2,1,0:T(8,128)S(1)} fusion(bf16[16,64,2176]{2,1,0:T(8,128)(2,1)} %copy-done.1, bf16[16,128,2176]{2,1,0:T(8,128)(2,1)} %bitcast.90), kind=kOutput, calls=%fused_computation.61.clone.1 | convolution fusion | flops 570425344 | bytes 13893632 | tf_op jit(solution)/shard_map/while/body/eval_jaxpr/dot_general | solution.py:45
  191.0 4.3 tile.11
  195.3 21.2 %tile.12 = bf16[16,278656]{1,0:T(8,128)(2,1)} reshape(bf16[16,128,2177]{2,1,0:T(8,128)(2,1)} %tile.11) | data formatting | bytes 17833984 | tf_op jit(solution)/shard_map/while/body/eval_jaxpr/vmap()/tile | solution.py:29
  216.5 7.4 %slice.146 = bf16[16,278528]{1,0:T(8,128)(2,1)} slice(bf16[16,278656]{1,0:T(8,128)(2,1)} %tile.12), slice={[0:16], [0:278528]} | slice | bytes 17825792 | tf_op jit(solution)/shard_map/while/body/eval_jaxpr/vmap()/slice | solution.py:29
  223.9 8.5 %copy.37 = bf16[2,8,128,2176]{3,2,1,0:T(8,128)(2,1)} copy(bf16[2,8,128,2176]{3,1,2,0:T(8,128)(2,1)} %bitcast.89) | data formatting | bytes 17825792 | tf_op jit(solution)/shard_map/while
  232.4 8.2 %fusion.39 = f32[16,64,128]{2,1,0:T(8,128)S(1)} fusion(bf16[16,64,2176]{2,1,0:T(8,128)(2,1)} %copy-done.1, bf16[16,128,2176]{2,1,0:T(8,128)(2,1)} %bitcast.90), kind=kOutput, calls=%fused_computation.61.clone.1 | convolution fusion | flops 570425344 | bytes 13893632 | tf_op jit(solution)/shard_map/while/body/eval_jaxpr/dot_general | solution.py:45
  248.8 215.3 %reduce-scatter.2.cloned.1.call-done = f32[128,128]{1,0:T(8,128)} async-done(((f32[4096,128]{1,0:T(8,128)}), f32[128,128]{1,0:T(8,128)}) %reduce-scatter.2.cloned.1.call-update) | async-done | bytes 65552 | tf_op jit(solution)/shard_map/reduce_scatter | solution.py:86
  475.1 69.6 %all-reduce.3.cloned.1.call-done = f32[4,128,128]{2,0,1:T(4,128)} async-done(((f32[4,128,128]{2,0,1:T(4,128)}), f32[4,128,128]{2,0,1:T(4,128)}) %all-reduce.3.cloned.1.call-update) | async-done | bytes 262160 | tf_op jit(solution)/shard_map/psum | solution.py:101
  (136 shorter events, 50.8 us)
Async XLA Ops:
  6.5 467.2 %copy-start = (f32[4,1,2]{0,2,1:T(2,128)S(1)}, f32[4,1,2]{0,2,1:T(2,128)}, u32[]{:S(2)}) copy-start(f32[4,1,2]{0,2,1:T(2,128)} %param.19) | copy-start | bytes 100
  6.5 457.5 %reduce-scatter.2.cloned.1.call-start = ((), (), s32[]{:S(2)}) async-start(), calls=%async_computation.1 | async-start | bytes 2162688 | tf_op jit(solution)/shard_map/reduce_scatter | solution.py:86
  7.5 7.0 %collective-permute-start = (bf16[1,64,1024]{2,1,0:T(8,128)(2,1)S(1)}, bf16[1,64,1024]{2,1,0:T(8,128)(2,1)S(1)}, u32[]{:S(2)}, u32[]{:S(2)}) collective-permute-start(bf16[1,64,1024]{2,1,0:T(8,128)(2,1)S(1)} %get-tuple-element.36), channel_id=1, source_target_pairs={{0,1},{1,2},{2,3},{3,4},{4,5},{5,6},{6,7},{7,8},{8,9},{9,10},{10,1... | collective-permute-start | bytes 393224 | tf_op jit(solution)/shard_map/ppermute | solution.py:19
  11.9 6.4 %collective-permute-start.1 = (bf16[1,64,1024]{2,1,0:T(8,128)(2,1)S(1)}, bf16[1,64,1024]{2,1,0:T(8,128)(2,1)S(1)}, u32[]{:S(2)}, u32[]{:S(2)}) collective-permute-start(bf16[1,64,1024]{2,1,0:T(8,128)(2,1)S(1)} %get-tuple-element.37), channel_id=1, source_target_pairs={{1,0},{2,1},{3,2},{4,3},{5,4},{6,5},{7,6},{8,7},{9,8},{10,9},{11,1... | collective-permute-start | bytes 393224 | tf_op jit(solution)/shard_map/ppermute | solution.py:20
  19.6 221.9 %copy-start.2 = (f32[1,64]{1,0:T(1,128)S(1)}, f32[1,64]{1,0:T(1,128)}, u32[]{:S(2)}) copy-start(f32[1,64]{1,0:T(1,128)} %param.13) | copy-start | bytes 772
  21.6 2.1 copy-start.1
  77.1 2.1 copy-start.1
  132.6 2.1 copy-start.1
  188.0 2.1 copy-start.1
  241.5 5.4 copy-start.3
  241.5 226.9 %copy-start.4 = (f32[1,2,33]{2,1,0:T(2,128)S(1)}, f32[1,2,33]{2,1,0:T(2,128)}, u32[]{:S(2)}) copy-start(f32[1,2,33]{2,1,0:T(2,128)} %param.18) | copy-start | bytes 796
  246.8 298.0 %all-reduce.3.cloned.1.call-start = ((), (), s32[]{:S(2)}) async-start(), calls=%async_computation.2 | async-start | bytes 524288 | tf_op jit(solution)/shard_map/psum | solution.py:101
  464.8 4.6 collective-permute-start.2
  467.1 5.1 collective-permute-start.3
Sparse Core Ops, SparseCore 0:
  246.9 217.0 reduce-scatter.1
  475.3 69.4 all-reduce.2
where the time goes:
time: 555 us; the launch traced here: 553 us
  waiting for transfers between devices  291 us (52%)
  local copies, waits for them, and re-layouts  192 us (35%)
  matrix products  43.6 us (8%)
  between operations  14.2 us (3%)
  starting transfers between devices  9.32 us (2%)
    reduce_scatter x1, waiting for transfers between devices, on_device(): lax.psum_scatter(jnp.dot(hits, block_vals, precision=lax.Precision.HIGHES...  215 us
    another operation x8, local copies, waits for them, and re-layouts, toeplitz_rows(): tiled = jnp.tile(padded_taps, seg_len)[:seg_len * width]  102 us
    psum x1, waiting for transfers between devices, on_device(): total = lax.psum(local_mix, 'band')  69.6 us
    while x84, local copies, waits for them, and re-layouts  49.5 us
    dot_general x4, matrix products, filter_group(): lax.dot_general(windows, tables, (((2,), (2,)), ((0,), (0,))), preferred_...  32.6 us
    slice x4, local copies, waits for them, and re-layouts, toeplitz_rows(): tiled = jnp.tile(padded_taps, seg_len)[:seg_len * width]  29.7 us
  transfers between devices with their start and end apart: 6, of which 4 were waited for; matrix products, arithmetic and copies ran while one was open for 1% of the time, Pallas kernels for 0%

commit v1 on v0

v1 whole, which is shorter than its diff:
```python
import functools

import jax
import jax.numpy as jnp
from jax import lax
from jax.experimental import pallas as pl
from jax.experimental.pallas import tpu as pltpu
from jax.sharding import PartitionSpec as P

PIX = 128
CAP = 8
HALF = 1024
LAGS = 16
BEAM = 33
REACH = 16
NBEAM = 2
NCOMP = 4
CHUNK = 1024
MESH = pl.DeviceIdType.MESH
F32 = jnp.float32
BF16 = jnp.bfloat16
NT = (((1,), (1,)), ((), ()))


def iota(shape, axis):
    return lax.broadcasted_iota(jnp.int32, shape, axis)


def split(value):
    high = value.astype(BF16)
    return high, (value - high.astype(F32)).astype(BF16)


def dot(a, b):
    return jnp.dot(a, b, preferred_element_type=F32)


def dot_nt(a, b):
    return lax.dot_general(a, b, NT, preferred_element_type=F32)


def lag_table(taps, weights, table):
    det = taps.shape[1]
    eye = iota((det, det), 0) == iota((det, det), 1)
    column = jnp.sum(jnp.where(eye, weights[0:1, :], 0.0), axis=1, keepdims=True)
    flip = jnp.where(iota((PIX, PIX), 0) + iota((PIX, PIX), 1) == PIX - 1, 1.0, 0.0).astype(BF16)
    pair = 2 * PIX
    for j in range(LAGS // 2):
        both = jnp.concatenate(
            [taps[0, :, pl.ds(pair * j + PIX * e, PIX)].astype(F32) * column for e in range(2)],
            axis=0,
        )
        high, low = split(both)
        lanes = pl.ds(2 * det * j, 2 * det)
        table[0:PIX, lanes] = dot_nt(flip, high).astype(BF16)
        table[PIX : 2 * PIX, lanes] = dot_nt(flip, low).astype(BF16)
    last = taps[0, :, 2 * HALF : 2 * HALF + 1].astype(F32) * column
    last_high = last.astype(BF16).astype(F32)
    spot = iota((det, 2 * det), 1) == iota((det, 2 * det), 0) + det
    row_high = jnp.sum(jnp.where(spot, last_high, 0.0), axis=0, keepdims=True)
    row_low = jnp.sum(jnp.where(spot, last - last_high, 0.0), axis=0, keepdims=True)
    rows = iota((16, 2 * det), 0)
    rest = (LAGS - 2) * det
    table[2 * PIX : 2 * PIX + 16, 0:rest] = jnp.zeros((16, rest), BF16)
    table[2 * PIX : 2 * PIX + 16, rest : rest + 2 * det] = jnp.where(
        rows == 0, row_high, jnp.where(rows == 1, row_low, 0.0)
    ).astype(BF16)


def filter_chunk(x, table, here, before, start, block, width):
    det = x.shape[0]
    total = None
    for q in range(LAGS // 4):
        window = jnp.concatenate(
            [x[:, pl.ds(start + PIX * (4 * q + e), width)] for e in range(4)], axis=0
        )
        part = dot(table[:, 4 * det * q : 4 * det * (q + 1)], window)
        total = part if total is None else total + part
    keeps = iota((PIX, PIX), 1) <= iota((PIX, PIX), 0)
    for k in range(width // PIX):
        lanes = slice(PIX * k, PIX * (k + 1))
        lagged = total[0:PIX, lanes] + total[PIX : 2 * PIX, lanes]
        turned = pltpu.roll(lagged, 1, 1, stride=1, stride_axis=0)
        final = total[2 * PIX : 2 * PIX + 1, lanes] + total[2 * PIX + 1 : 2 * PIX + 2, lanes]
        here[pl.ds(block + k, 1), :] = jnp.sum(
            jnp.where(keeps, turned, 0.0), axis=0, keepdims=True
        )
        before[pl.ds(block + k, 1), :] = (
            jnp.sum(jnp.where(keeps, 0.0, turned), axis=0, keepdims=True) + final
        )


def band_rows(profile, out_rows, shift):
    wide = jnp.concatenate([profile, jnp.zeros((1, PIX - BEAM), F32)], axis=1)
    spread = jnp.broadcast_to(wide, (out_rows, PIX))
    turned = pltpu.roll(spread, PIX - shift, 1, stride=1, stride_axis=0)
    tap = iota((out_rows, PIX), 1) - iota((out_rows, PIX), 0) + shift
    return jnp.where((tap >= 0) & (tap < BEAM), turned, 0.0)


def kernel(
    bands,
    shards,
    side,
    tod,
    taps,
    weights,
    owner,
    tile_row,
    counts,
    beam_rows,
    beam_cols,
    mixing,
    out,
    x,
    table,
    here,
    before,
    meta_out,
    meta_in,
    vals_out,
    vals_in,
    mix_out,
    mix_in,
    wide,
    mine,
    edge,
    load_sem,
    halo_send,
    halo_recv,
    peer_send,
    peer_recv,
    band_send,
    band_recv,
    edge_send,
    edge_recv,
):
    band = lax.axis_index("band")
    shard = lax.axis_index("tm")
    depth = shards // side
    sx, sz = lax.div(shard, side), lax.rem(shard, side)
    samples = tod.shape[2]
    blocks = samples // PIX
    share = REACH
    span = bands * share
    has_left, has_right = shard > 0, shard < shards - 1
    left, right = lax.rem(shard + shards - 1, shards), lax.rem(shard + 1, shards)

    def shard_peer(i):
        return lax.rem(sx + i // side, depth) * side + lax.rem(sz + i % side, side)

    def hops(i):
        dx, dz = i // side, i % side
        return min(dx, depth - dx) + min(dz, side - dz)

    order = sorted(range(1, shards), key=lambda i: -hops(i))

    barrier = pltpu.get_barrier_semaphore()
    for i in order:
        pl.semaphore_signal(barrier, 1, device_id=(band, shard_peer(i)), device_id_type=MESH)
    for i in range(1, bands):
        pl.semaphore_signal(barrier, 1, device_id=(lax.rem(band + i, bands), shard), device_id_type=MESH)

    @pl.when((band == 0) & has_left)
    def _():
        for b in range(1, bands):
            pl.semaphore_signal(barrier, 1, device_id=(b, left), device_id_type=MESH)

    @pl.when((band == bands - 1) & has_right)
    def _():
        for b in range(bands - 1):
            pl.semaphore_signal(barrier, 1, device_id=(b, right), device_id_type=MESH)

    load = pltpu.make_async_copy(tod.at[0], x.at[:, pl.ds(HALF, samples)], load_sem)
    load.start()

    row_i, lane_i = iota((blocks, blocks), 0), iota((blocks, blocks), 1)
    diagonal = row_i == lane_i
    owner_col = owner[0]
    owner_row = jnp.sum(jnp.where(diagonal, owner_col, 0), axis=0, keepdims=True)
    same = (owner_col == owner_row) & (row_i < lane_i)
    rank_row = jnp.sum(jnp.where(same, 1, 0), axis=0, keepdims=True)
    ox, oz = owner_row // side, owner_row % side
    group = ((ox - sx + depth) % depth) * side + (oz - sz + side) % side
    slot_row = group * CAP + rank_row
    kept = iota((1, blocks), 1) < counts[0:1, 0:1]
    slots = shards * CAP
    pick = jnp.where((iota((slots, blocks), 0) == slot_row) & kept, 1.0, 0.0).astype(BF16)
    row_col = jnp.sum(jnp.where(diagonal, tile_row[0:1, :], 0), axis=1, keepdims=True)
    row_hot = jnp.where(iota((blocks, PIX), 1) == row_col, 1.0, 0.0).astype(BF16)
    meta = dot(pick, row_hot)
    meta_out[...] = meta
    meta_in[0:CAP, :] = meta[0:CAP, :]
    mix_row = iota((NCOMP * NBEAM, PIX), 0)
    mix = jnp.zeros((NCOMP * NBEAM, PIX), F32)
    for c in range(NCOMP):
        for k in range(NBEAM):
            mix = jnp.where(mix_row == c * NBEAM + k, mixing[c, 0, k], mix)
    mix_out[...] = mix
    mix_in[0] = mix

    lag_table(taps, weights, table)
    load.wait()

    def chunk_step(index, carry):
        start = pl.multiple_of(index * CHUNK, PIX)
        filter_chunk(x, table, here, before, start, index * (CHUNK // PIX), CHUNK)
        return carry

    lax.fori_loop(1, 3, chunk_step, 0)

    pl.semaphore_wait(
        barrier,
        shards
        - 1
        + bands
        - 1
        + jnp.where((band != 0) & has_right, 1, 0)
        + jnp.where((band != bands - 1) & has_left, 1, 0),
    )

    to_right = pltpu.make_async_remote_copy(
        x.at[:, pl.ds(samples, HALF)],
        x.at[:, pl.ds(0, HALF)],
        halo_send.at[0],
        halo_recv.at[0],
        device_id=(band, right),
        device_id_type=MESH,
    )
    to_left = pltpu.make_async_remote_copy(
        x.at[:, pl.ds(HALF, HALF)],
        x.at[:, pl.ds(samples + HALF, HALF)],
        halo_send.at[1],
        halo_recv.at[1],
        device_id=(band, left),
        device_id_type=MESH,
    )

    @pl.when(has_right)
    def _():
        to_right.start()

    @pl.when(has_left)
    def _():
        to_left.start()

    def to_shards(source, target, which):
        for i in order:
            pltpu.make_async_remote_copy(
                source.at[pl.ds(CAP * i, CAP)],
                target.at[pl.ds(CAP * i, CAP)],
                peer_send.at[which],
                peer_recv.at[which],
                device_id=(band, shard_peer(i)),
                device_id_type=MESH,
            ).start()

    def from_shards(ref, sem):
        part = ref.at[pl.ds(CAP, slots - CAP)]
        pltpu.make_async_copy(part, part, sem).wait()

    to_shards(meta_out, meta_in, 0)
    for i in range(1, bands):
        pltpu.make_async_remote_copy(
            mix_out,
            mix_in.at[i],
            band_send.at[0, i],
            band_recv.at[0, i],
            device_id=(lax.rem(band + i, bands), shard),
            device_id_type=MESH,
        ).start()

    lax.fori_loop(3, 7, chunk_step, 0)

    @pl.when(has_left)
    def _():
        part = x.at[:, pl.ds(0, HALF)]
        pltpu.make_async_copy(part, part, halo_recv.at[0]).wait()

    @pl.when(jnp.logical_not(has_left))
    def _():
        x[:, 0:HALF] = jnp.zeros((x.shape[0], HALF), BF16)

    @pl.when(has_right)
    def _():
        part = x.at[:, pl.ds(samples + HALF, HALF)]
        pltpu.make_async_copy(part, part, halo_recv.at[1]).wait()

    @pl.when(jnp.logical_not(has_right))
    def _():
        x[:, pl.ds(samples + HALF, HALF)] = jnp.zeros((x.shape[0], HALF), BF16)

    for index in (samples // CHUNK - 1, 0):
        filter_chunk(
            x, table, here, before, index * CHUNK, index * (CHUNK // PIX), CHUNK
        )
    filter_chunk(x, table, here, before, samples, blocks, PIX)

    block_values = here[0:blocks, :] + before[pl.ds(1, blocks), :]
    value_high, value_low = split(block_values)
    values = dot(pick, value_high) + dot(pick, value_low)
    vals_out[...] = values
    vals_in[0:CAP, :] = values[0:CAP, :]
    to_shards(vals_out, vals_in, 1)

    long = span + 2 * REACH
    row_mats = jnp.concatenate(
        [band_rows(beam_rows[0, k : k + 1, :], long, BEAM - 1) for k in range(NBEAM)],
        axis=0,
    )
    rows_high, rows_low = split(row_mats)
    from_shards(meta_in, peer_recv.at[0])
    hot = meta_in[...].astype(BF16)
    slot_high = dot_nt(rows_high, hot).astype(BF16)
    slot_low = dot_nt(rows_low, hot).astype(BF16)
    cols = [split(band_rows(beam_cols[0, k : k + 1, :], PIX, REACH)) for k in range(NBEAM)]

    from_shards(vals_in, peer_recv.at[1])
    in_high, in_low = split(vals_in[...])
    rowed = dot(slot_high, in_high) + dot(slot_high, in_low) + dot(slot_low, in_high)
    for k in range(NBEAM):
        rowed_high, rowed_low = split(rowed[long * k : long * (k + 1), :])
        col_high, col_low = cols[k]
        wide[k] = (
            dot_nt(rowed_high, col_high) + dot_nt(rowed_low, col_high) + dot_nt(rowed_high, col_low)
        )

    below = pltpu.make_async_remote_copy(
        wide.at[:, pl.ds(REACH + span, REACH), :],
        edge.at[lax.rem(bands - band, bands)],
        edge_send.at[0],
        edge_recv.at[lax.rem(bands - band, bands)],
        device_id=(0, right),
        device_id_type=MESH,
    )
    above = pltpu.make_async_remote_copy(
        wide.at[:, pl.ds(0, REACH), :],
        edge.at[bands - 1 - band],
        edge_send.at[1],
        edge_recv.at[bands - 1 - band],
        device_id=(bands - 1, left),
        device_id_type=MESH,
    )

    @pl.when(has_right)
    def _():
        below.start()

    @pl.when(has_left)
    def _():
        above.start()

    sends = []
    for i in range(1, bands):
        peer = lax.rem(band + i, bands)
        copy = pltpu.make_async_remote_copy(
            wide.at[:, pl.ds(pl.multiple_of(REACH + share * peer, REACH), share), :],
            mine.at[i],
            band_send.at[1, i],
            band_recv.at[1, i],
            device_id=(peer, shard),
            device_id_type=MESH,
        )
        copy.start()
        sends.append(copy)
    mine[0] = wide[:, pl.ds(pl.multiple_of(REACH + share * band, REACH), share), :]
    for i in range(1, bands):
        pltpu.make_async_copy(mix_in.at[i], mix_in.at[i], band_recv.at[0, i]).wait()
    for i in range(1, bands):
        pltpu.make_async_copy(mine.at[i], mine.at[i], band_recv.at[1, i]).wait()

    @pl.when(((band == 0) & has_left) | ((band == bands - 1) & has_right))
    def _():
        for i in range(bands):
            pltpu.make_async_copy(edge.at[i], edge.at[i], edge_recv.at[i]).wait()
        mine[...] += edge[...]

    for c in range(NCOMP):
        total = None
        for i in range(bands):
            for k in range(NBEAM):
                term = mix_in[i, c * NBEAM + k : c * NBEAM + k + 1, :] * mine[i, k]
                total = term if total is None else total + term
        out[c, 0] = total

    @pl.when(has_right)
    def _():
        to_right.wait_send()
        below.wait_send()

    @pl.when(has_left)
    def _():
        to_left.wait_send()
        above.wait_send()

    from_shards(meta_out, peer_send.at[0])
    from_shards(vals_out, peer_send.at[1])
    for i in range(1, bands):
        pltpu.make_async_copy(mix_out, mix_out, band_send.at[0, i]).wait()
    for copy in sends:
        copy.wait_send()


def on_device(
    tod, filter_taps, det_weights, owner, tile_row, block_counts, beam_rows, beam_cols, mixing
):
    bands, shards = lax.axis_size("band"), lax.axis_size("tm")
    side = 8 if shards >= 16 else shards // 2
    det, samples = tod.shape[1:]
    slots = shards * CAP
    long = bands * REACH + 2 * REACH
    blocks = samples // PIX
    vmem = pl.BlockSpec(memory_space=pltpu.VMEM)
    return pl.pallas_call(
        functools.partial(kernel, bands, shards, side),
        out_shape=jax.ShapeDtypeStruct((NCOMP, 1, REACH, PIX), F32),
        in_specs=[pl.BlockSpec(memory_space=pl.ANY)]
        + [vmem] * 7
        + [pl.BlockSpec(memory_space=pltpu.SMEM)],
        out_specs=vmem,
        scratch_shapes=[
            pltpu.VMEM((det, samples + 2 * HALF), BF16),
            pltpu.VMEM((2 * PIX + 16, LAGS * det), BF16),
            pltpu.VMEM((blocks + 8, PIX), F32),
            pltpu.VMEM((blocks + 8, PIX), F32),
            pltpu.VMEM((slots, PIX), F32),
            pltpu.VMEM((slots, PIX), F32),
            pltpu.VMEM((slots, PIX), F32),
            pltpu.VMEM((slots, PIX), F32),
            pltpu.VMEM((NCOMP * NBEAM, PIX), F32),
            pltpu.VMEM((bands, NCOMP * NBEAM, PIX), F32),
            pltpu.VMEM((NBEAM, long, PIX), F32),
            pltpu.VMEM((bands, NBEAM, REACH, PIX), F32),
            pltpu.VMEM((bands, NBEAM, REACH, PIX), F32),
            pltpu.SemaphoreType.DMA,
            pltpu.SemaphoreType.DMA((2,)),
            pltpu.SemaphoreType.DMA((2,)),
            pltpu.SemaphoreType.DMA((2,)),
            pltpu.SemaphoreType.DMA((2,)),
            pltpu.SemaphoreType.DMA((2, bands)),
            pltpu.SemaphoreType.DMA((2, bands)),
            pltpu.SemaphoreType.DMA((2,)),
            pltpu.SemaphoreType.DMA((bands,)),
        ],
        compiler_params=pltpu.CompilerParams(
            collective_id=0, has_side_effects=True, vmem_limit_bytes=48 * 2**20
        ),
    )(tod, filter_taps, det_weights, owner, tile_row, block_counts, beam_rows, beam_cols, mixing)


def solution(mesh):
    placed = (
        P("band", None, "tm"),
        P("band", None, None),
        P("band", None),
        P("band", "tm", None),
        P("band", "tm"),
        P("band", "tm"),
        P("band", None, None),
        P("band", None, None),
        P(None, "band", None),
    )
    return jax.shard_map(
        on_device,
        mesh=mesh,
        in_specs=placed,
        out_specs=P(None, "tm", "band", None),
        check_vma=False,
    )
```

time: 555 us -> 36.3 us (0.07)
  waiting for transfers between devices: 291 us -> 0 us
  local copies, waits for them, and re-layouts: 192 us -> 4.15 us
  matrix products: 43.6 us -> 0 us
  Pallas kernels: 0 us -> 31.3 us
  between operations: 14.2 us -> 0.69 us
  starting transfers between devices: 9.32 us -> 0 us
    reduce_scatter x1 -> x0, waiting for transfers between devices: 215 us -> none  [on_device(): lax.psum_scatter(jnp.dot(hits, block_vals, precision=lax.Precision.HIGHES...]
    another operation x8 -> x0, local copies, waits for them, and re-layouts: 102 us -> none  [toeplitz_rows(): tiled = jnp.tile(padded_taps, seg_len)[:seg_len * width]]
    psum x1 -> x0, waiting for transfers between devices: 69.6 us -> none  [on_device(): total = lax.psum(local_mix, 'band')]
    while x84 -> x0, local copies, waits for them, and re-layouts: 49.5 us -> none
    dot_general x11 -> x0, matrix products: 43.6 us -> none  [the longest x4 32.6 us: filter_group(): lax.dot_general(windows, tables, (((2,), (2,)), ((0,), (0,))), preferred_...]
    slice x6 -> x0, local copies, waits for them, and re-layouts: 31.4 us -> none  [the longest x4 29.7 us: toeplitz_rows(): tiled = jnp.tile(padded_taps, seg_len)[:seg_len * width]]
    pallas_call x0 -> x1, Pallas kernels: none -> 31.3 us  [on_device(): pl.pallas_call(functools.partial(kernel, bands, shards, side), out_shape=...]
    ppermute x4 -> x0, starting transfers between devices: 9.28 us -> none  [the longest x2 6.7 us: with_halo(): before = lax.ppermute(last, axis, up)]
  transfers between devices with their start and end apart: 6 -> 0, of which waited for: 4 -> 0; matrix products, arithmetic and copies ran while one was open for 1% -> 0% of each run, Pallas kernels for 0% -> 0%
where the time goes in v1:
time: 36.3 us; the launch traced here: 36.1 us
  Pallas kernels  31.3 us (86%)
  local copies, waits for them, and re-layouts  4.15 us (11%)
  between operations  0.69 us (2%)
    pallas_call x1, Pallas kernels, on_device(): pl.pallas_call(functools.partial(kernel, bands, shards, side), out_shape=...  31.3 us
    unnamed x19, local copies, waits for them, and re-layouts  4.15 us

profile of v1, /device:TPU:1, one launch (start us, length us, event | category | flops | bytes accessed | tf_op | source)
XLA Modules:
  0.0 36.1 jit_solution(12365836128468226234)
XLA Ops:
  0.0 0.0 copy-start.6
  0.7 0.0 copy-done.6
  0.7 0.0 copy-start.7
  0.7 0.1 copy.11.mixing
  0.8 0.6 %copy-done.7 = s32[1,64,1]{1,2,0:T(1,128)S(1)} copy-done((s32[1,64,1]{1,2,0:T(1,128)S(1)}, s32[1,64,1]{1,2,0:T(1,128)}, u32[]{:S(2)}) %copy-start.7) | copy-done | bytes 280
  1.3 0.0 copy-start.2
  1.3 0.0 copy-start.3
  1.3 0.0 copy-start.4
  1.3 0.0 copy-start.5
  1.3 0.1 copy.10.owner
  1.4 0.6 %copy-done.2 = f32[1,2,33]{2,1,0:T(2,128)S(1)} copy-done((f32[1,2,33]{2,1,0:T(2,128)S(1)}, f32[1,2,33]{2,1,0:T(2,128)}, u32[]{:S(2)}) %copy-start.2) | copy-done | bytes 288
  2.0 0.0 copy-done.3
  2.0 0.0 copy-done.4
  2.0 0.0 copy-done.5
  2.0 0.0 copy-start
  2.0 1.2 %copy-done = bf16[1,64,8192]{2,1,0:T(8,128)(2,1)S(1)} copy-done((bf16[1,64,8192]{2,1,0:T(8,128)(2,1)S(1)}, bf16[1,64,8192]{2,1,0:T(8,128)(2,1)}, u32[]{:S(2)}) %copy-start) | copy-done | bytes 1048600
  3.3 0.0 copy-start.1
  3.3 1.0 %copy-done.1 = bf16[1,64,2049]{2,1,0:T(8,128)(2,1)S(1)} copy-done((bf16[1,64,2049]{2,1,0:T(8,128)(2,1)S(1)}, bf16[1,64,2049]{2,1,0:T(8,128)(2,1)}, u32[]{:S(2)}) %copy-start.1) | copy-done | bytes 262296
  4.2 31.3 %shard_map.91 = f32[4,1,16,128]{3,2,1,0:T(8,128)S(1)} custom-call(bf16[1,64,8192]{2,1,0:T(8,128)(2,1)S(1)} %copy-done, bf16[1,64,2049]{2,1,0:T(8,128)(2,1)S(1)} %copy-done.1, f32[1,64]{1,0:T(1,128)S(1)} %copy-done.4, s32[1,64,1]{2,1,0:T(8,128)S(1)} %copy.10.owner, s32[1,64]{1,0:T(1,128)S(1)} %copy-done.5, s32[1,1]{1,0:T(1,128)S(6)} %copy.13.counts, ...), custom_call_target="tpu_custom_call" | custom-call | tf_op jit(solution)/shard_map/pallas_call | solution.py:414
  35.5 0.6 %copy.14 = f32[4,1,16,128]{3,2,1,0:T(8,128)} copy(f32[4,1,16,128]{3,2,1,0:T(8,128)S(1)} %shard_map.91) | data formatting | bytes 65536
Async XLA Ops:
  0.0 0.7 %copy-start.6 = (f32[4,1,2]{0,2,1:T(2,128)S(1)}, f32[4,1,2]{0,2,1:T(2,128)}, u32[]{:S(2)}) copy-start(f32[4,1,2]{0,2,1:T(2,128)} %param.17) | copy-start | bytes 100
  0.7 0.7 %copy-start.7 = (s32[1,64,1]{1,2,0:T(1,128)S(1)}, s32[1,64,1]{1,2,0:T(1,128)}, u32[]{:S(2)}) copy-start(s32[1,64,1]{1,2,0:T(1,128)} %param.12) | copy-start | bytes 772
  1.3 0.7 %copy-start.2 = (f32[1,2,33]{2,1,0:T(2,128)S(1)}, f32[1,2,33]{2,1,0:T(2,128)}, u32[]{:S(2)}) copy-start(f32[1,2,33]{2,1,0:T(2,128)} %beam_rows.1) | copy-start | bytes 796
  1.3 0.7 %copy-start.3 = (f32[1,2,33]{2,1,0:T(2,128)S(1)}, f32[1,2,33]{2,1,0:T(2,128)}, u32[]{:S(2)}) copy-start(f32[1,2,33]{2,1,0:T(2,128)} %beam_cols.1) | copy-start | bytes 796
  1.3 0.7 %copy-start.4 = (f32[1,64]{1,0:T(1,128)S(1)}, f32[1,64]{1,0:T(1,128)}, u32[]{:S(2)}) copy-start(f32[1,64]{1,0:T(1,128)} %weights.1) | copy-start | bytes 772
  1.3 0.7 %copy-start.5 = (s32[1,64]{1,0:T(1,128)S(1)}, s32[1,64]{1,0:T(1,128)}, u32[]{:S(2)}) copy-start(s32[1,64]{1,0:T(1,128)} %tile_row.1) | copy-start | bytes 772
  2.0 1.2 %copy-start = (bf16[1,64,8192]{2,1,0:T(8,128)(2,1)S(1)}, bf16[1,64,8192]{2,1,0:T(8,128)(2,1)}, u32[]{:S(2)}) copy-start(bf16[1,64,8192]{2,1,0:T(8,128)(2,1)} %tod.1) | copy-start | bytes 3145732
  3.3 1.0 %copy-start.1 = (bf16[1,64,2049]{2,1,0:T(8,128)(2,1)S(1)}, bf16[1,64,2049]{2,1,0:T(8,128)(2,1)}, u32[]{:S(2)}) copy-start(bf16[1,64,2049]{2,1,0:T(8,128)(2,1)} %taps.1) | copy-start | bytes 786820

commit v2 on v1

--- a/solution.py
+++ b/solution.py
@@ -16,6 +16,8 @@
 NBEAM = 2
 NCOMP = 4
 CHUNK = 1024
+STEP = CHUNK // PIX
+ALL = (0, 1, 2, 3)
 MESH = pl.DeviceIdType.MESH
 F32 = jnp.float32
 BF16 = jnp.bfloat16
@@ -67,27 +69,41 @@
     ).astype(BF16)
 
 
-def filter_chunk(x, table, here, before, start, block, width):
+def lagged_sums(x, table, block, parts):
     det = x.shape[0]
     total = None
-    for q in range(LAGS // 4):
+    for q in parts:
         window = jnp.concatenate(
-            [x[:, pl.ds(start + PIX * (4 * q + e), width)] for e in range(4)], axis=0
+            [
+                x[:, pl.ds(pl.multiple_of(PIX * block, PIX) + PIX * (4 * q + e), CHUNK)]
+                for e in range(4)
+            ],
+            axis=0,
         )
         part = dot(table[:, 4 * det * q : 4 * det * (q + 1)], window)
         total = part if total is None else total + part
+    return total
+
+
+def add_diagonals(sums, here, before, block):
     keeps = iota((PIX, PIX), 1) <= iota((PIX, PIX), 0)
-    for k in range(width // PIX):
-        lanes = slice(PIX * k, PIX * (k + 1))
-        lagged = total[0:PIX, lanes] + total[PIX : 2 * PIX, lanes]
-        turned = pltpu.roll(lagged, 1, 1, stride=1, stride_axis=0)
-        final = total[2 * PIX : 2 * PIX + 1, lanes] + total[2 * PIX + 1 : 2 * PIX + 2, lanes]
-        here[pl.ds(block + k, 1), :] = jnp.sum(
-            jnp.where(keeps, turned, 0.0), axis=0, keepdims=True
+    prior = None
+    for k in range(STEP):
+        lanes = pl.ds(PIX * k, PIX)
+        turned = pltpu.roll(
+            sums[0:PIX, lanes] + sums[PIX : 2 * PIX, lanes], 1, 1, stride=1, stride_axis=0
         )
-        before[pl.ds(block + k, 1), :] = (
-            jnp.sum(jnp.where(keeps, 0.0, turned), axis=0, keepdims=True) + final
-        )
+        final = sums[2 * PIX : 2 * PIX + 1, lanes] + sums[2 * PIX + 1 : 2 * PIX + 2, lanes]
+        merged = jnp.where(keeps, 0.0 if k == 0 else prior, turned)
+        done = jnp.sum(merged, axis=0, keepdims=True) + final
+        if k == 0:
+            before[pl.ds(block, 1), :] = done
+        else:
+            here[pl.ds(block + k - 1, 1), :] = done
+        prior = turned
+    here[pl.ds(block + STEP - 1, 1), :] = jnp.sum(
+        jnp.where(keeps, prior, 0.0), axis=0, keepdims=True
+    )
 
 
 def band_rows(profile, out_rows, shift):
@@ -103,6 +119,15 @@
     shards,
     side,
     tod,
+    taps_hbm,
+    weights_hbm,
+    owner_hbm,
+    tile_row_hbm,
+    counts_hbm,
+    beam_rows_hbm,
+    beam_cols_hbm,
+    mixing_hbm,
+    out,
     taps,
     weights,
     owner,
@@ -111,11 +136,14 @@
     beam_rows,
     beam_cols,
     mixing,
-    out,
     x,
     table,
     here,
     before,
+    even,
+    odd,
+    overhang,
+    arrived,
     meta_out,
     meta_in,
     vals_out,
@@ -126,6 +154,7 @@
     mine,
     edge,
     load_sem,
+    small_sem,
     halo_send,
     halo_recv,
     peer_send,
@@ -153,6 +182,24 @@
         dx, dz = i // side, i % side
         return min(dx, depth - dx) + min(dz, side - dz)
 
+    loads = []
+    for n, (source, target) in enumerate(
+        (
+            (owner_hbm, owner),
+            (tile_row_hbm, tile_row),
+            (counts_hbm, counts),
+            (mixing_hbm, mixing),
+            (weights_hbm, weights),
+            (taps_hbm, taps),
+            (beam_rows_hbm, beam_rows),
+            (beam_cols_hbm, beam_cols),
+        )
+    ):
+        loads.append(pltpu.make_async_copy(source, target, small_sem.at[n]))
+        loads[-1].start()
+    load = pltpu.make_async_copy(tod.at[0], x.at[:, pl.ds(2 * HALF, samples)], load_sem)
+    load.start()
+
     order = sorted(range(1, shards), key=lambda i: -hops(i))
 
     barrier = pltpu.get_barrier_semaphore()
@@ -171,13 +218,16 @@
         for b in range(bands - 1):
             pl.semaphore_signal(barrier, 1, device_id=(b, right), device_id_type=MESH)
 
-    load = pltpu.make_async_copy(tod.at[0], x.at[:, pl.ds(HALF, samples)], load_sem)
-    load.start()
+    before[...] = jnp.zeros_like(before)
+    for start in (0, samples + 2 * HALF):
+        x[:, pl.ds(start, 2 * HALF)] = jnp.zeros((x.shape[0], 2 * HALF), BF16)
 
     row_i, lane_i = iota((blocks, blocks), 0), iota((blocks, blocks), 1)
     diagonal = row_i == lane_i
-    owner_col = owner[0]
-    owner_row = jnp.sum(jnp.where(diagonal, owner_col, 0), axis=0, keepdims=True)
+    for copy in loads[:4]:
+        copy.wait()
+    owner_row = owner[0:1, :]
+    owner_col = jnp.sum(jnp.where(diagonal, owner_row, 0), axis=1, keepdims=True)
     same = (owner_col == owner_row) & (row_i < lane_i)
     rank_row = jnp.sum(jnp.where(same, 1, 0), axis=0, keepdims=True)
     ox, oz = owner_row // side, owner_row % side
@@ -191,23 +241,32 @@
     meta = dot(pick, row_hot)
     meta_out[...] = meta
     meta_in[0:CAP, :] = meta[0:CAP, :]
-    mix_row = iota((NCOMP * NBEAM, PIX), 0)
-    mix = jnp.zeros((NCOMP * NBEAM, PIX), F32)
-    for c in range(NCOMP):
-        for k in range(NBEAM):
-            mix = jnp.where(mix_row == c * NBEAM + k, mixing[c, 0, k], mix)
+    mix = jnp.concatenate(
+        [jnp.broadcast_to(mixing[0, :, c : c + 1], (NBEAM, PIX)) for c in range(NCOMP)], axis=0
+    )
     mix_out[...] = mix
     mix_in[0] = mix
 
+    for copy in loads[4:]:
+        copy.wait()
     lag_table(taps, weights, table)
     load.wait()
 
-    def chunk_step(index, carry):
-        start = pl.multiple_of(index * CHUNK, PIX)
-        filter_chunk(x, table, here, before, start, index * (CHUNK // PIX), CHUNK)
+    even[...] = lagged_sums(x, table, blocks + STEP, (0, 1))
+    odd[...] = lagged_sums(x, table, 0, (2, 3))
+    add_diagonals(even, here, before, blocks + STEP)
+
+    def two_chunks(i, carry):
+        block = pl.multiple_of(STEP + 2 * STEP * i, STEP)
+        even[...] = lagged_sums(x, table, block, ALL)
+        add_diagonals(odd, here, before, pl.multiple_of(block - STEP, STEP))
+        odd[...] = lagged_sums(x, table, pl.multiple_of(block + STEP, STEP), ALL)
+        add_diagonals(even, here, before, block)
         return carry
 
-    lax.fori_loop(1, 3, chunk_step, 0)
+    lax.fori_loop(0, 2, two_chunks, 0)
+    overhang[0] = here[0:STEP, :] + before[pl.ds(1, STEP), :]
+    overhang[1] = here[pl.ds(blocks + STEP, STEP), :] + before[pl.ds(blocks + STEP + 1, STEP), :]
 
     pl.semaphore_wait(
         barrier,
@@ -219,20 +278,20 @@
         + jnp.where((band != bands - 1) & has_left, 1, 0),
     )
 
+    to_left = pltpu.make_async_remote_copy(
+        overhang.at[0],
+        arrived.at[1],
+        halo_send.at[0],
+        halo_recv.at[1],
+        device_id=(band, left),
+        device_id_type=MESH,
+    )
     to_right = pltpu.make_async_remote_copy(
-        x.at[:, pl.ds(samples, HALF)],
-        x.at[:, pl.ds(0, HALF)],
-        halo_send.at[0],
+        overhang.at[1],
+        arrived.at[0],
+        halo_send.at[1],
         halo_recv.at[0],
         device_id=(band, right),
-        device_id_type=MESH,
-    )
-    to_left = pltpu.make_async_remote_copy(
-        x.at[:, pl.ds(HALF, HALF)],
-        x.at[:, pl.ds(samples + HALF, HALF)],
-        halo_send.at[1],
-        halo_recv.at[1],
-        device_id=(band, left),
         device_id_type=MESH,
     )
 
@@ -270,33 +329,25 @@
             device_id_type=MESH,
         ).start()
 
-    lax.fori_loop(3, 7, chunk_step, 0)
-
-    @pl.when(has_left)
-    def _():
-        part = x.at[:, pl.ds(0, HALF)]
-        pltpu.make_async_copy(part, part, halo_recv.at[0]).wait()
-
-    @pl.when(jnp.logical_not(has_left))
-    def _():
-        x[:, 0:HALF] = jnp.zeros((x.shape[0], HALF), BF16)
-
-    @pl.when(has_right)
-    def _():
-        part = x.at[:, pl.ds(samples + HALF, HALF)]
-        pltpu.make_async_copy(part, part, halo_recv.at[1]).wait()
-
-    @pl.when(jnp.logical_not(has_right))
-    def _():
-        x[:, pl.ds(samples + HALF, HALF)] = jnp.zeros((x.shape[0], HALF), BF16)
-
-    for index in (samples // CHUNK - 1, 0):
-        filter_chunk(
-            x, table, here, before, index * CHUNK, index * (CHUNK // PIX), CHUNK
-        )
-    filter_chunk(x, table, here, before, samples, blocks, PIX)
-
-    block_values = here[0:blocks, :] + before[pl.ds(1, blocks), :]
+    lax.fori_loop(2, blocks // (2 * STEP), two_chunks, 0)
+    add_diagonals(odd, here, before, blocks)
+
+    for side_of, exists in enumerate((has_left, has_right)):
+
+        @pl.when(exists)
+        def _(side_of=side_of):
+            part = arrived.at[side_of]
+            pltpu.make_async_copy(part, part, halo_recv.at[side_of]).wait()
+
+        @pl.when(jnp.logical_not(exists))
+        def _(side_of=side_of):
+            arrived[side_of] = jnp.zeros((STEP, PIX), F32)
+
+    own = here[pl.ds(STEP, blocks), :] + before[pl.ds(STEP + 1, blocks), :]
+    block_values = jnp.concatenate(
+        [own[0:STEP] + arrived[0], own[STEP : blocks - STEP], own[blocks - STEP :] + arrived[1]],
+        axis=0,
+    )
     value_high, value_low = split(block_values)
     values = dot(pick, value_high) + dot(pick, value_low)
     vals_out[...] = values
@@ -414,15 +465,25 @@
     return pl.pallas_call(
         functools.partial(kernel, bands, shards, side),
         out_shape=jax.ShapeDtypeStruct((NCOMP, 1, REACH, PIX), F32),
-        in_specs=[pl.BlockSpec(memory_space=pl.ANY)]
-        + [vmem] * 7
-        + [pl.BlockSpec(memory_space=pltpu.SMEM)],
+        in_specs=[pl.BlockSpec(memory_space=pltpu.HBM)] * 9,
         out_specs=vmem,
         scratch_shapes=[
-            pltpu.VMEM((det, samples + 2 * HALF), BF16),
+            pltpu.VMEM(filter_taps.shape, BF16),
+            pltpu.VMEM((1, det), F32),
+            pltpu.VMEM((1, blocks), jnp.int32),
+            pltpu.VMEM((1, blocks), jnp.int32),
+            pltpu.VMEM((1, 1), jnp.int32),
+            pltpu.VMEM(beam_rows.shape, F32),
+            pltpu.VMEM(beam_cols.shape, F32),
+            pltpu.VMEM((1, NBEAM, NCOMP), F32),
+            pltpu.VMEM((det, samples + 4 * HALF), BF16),
             pltpu.VMEM((2 * PIX + 16, LAGS * det), BF16),
-            pltpu.VMEM((blocks + 8, PIX), F32),
-            pltpu.VMEM((blocks + 8, PIX), F32),
+            pltpu.VMEM((blocks + 3 * STEP, PIX), F32),
+            pltpu.VMEM((blocks + 3 * STEP, PIX), F32),
+            pltpu.VMEM((2 * PIX + 16, CHUNK), F32),
+            pltpu.VMEM((2 * PIX + 16, CHUNK), F32),
+            pltpu.VMEM((2, STEP, PIX), F32),
+            pltpu.VMEM((2, STEP, PIX), F32),
             pltpu.VMEM((slots, PIX), F32),
             pltpu.VMEM((slots, PIX), F32),
             pltpu.VMEM((slots, PIX), F32),
@@ -433,6 +494,7 @@
             pltpu.VMEM((bands, NBEAM, REACH, PIX), F32),
             pltpu.VMEM((bands, NBEAM, REACH, PIX), F32),
             pltpu.SemaphoreType.DMA,
+            pltpu.SemaphoreType.DMA((8,)),
             pltpu.SemaphoreType.DMA((2,)),
             pltpu.SemaphoreType.DMA((2,)),
             pltpu.SemaphoreType.DMA((2,)),
@@ -443,9 +505,19 @@
             pltpu.SemaphoreType.DMA((bands,)),
         ],
         compiler_params=pltpu.CompilerParams(
-            collective_id=0, has_side_effects=True, vmem_limit_bytes=48 * 2**20
+            collective_id=0, has_side_effects=True, vmem_limit_bytes=67043328
         ),
-    )(tod, filter_taps, det_weights, owner, tile_row, block_counts, beam_rows, beam_cols, mixing)
+    )(
+        tod,
+        filter_taps,
+        det_weights,
+        owner.reshape(1, blocks),
+        tile_row,
+        block_counts,
+        beam_rows,
+        beam_cols,
+        mixing.transpose(1, 2, 0),
+    )
 
 
 def solution(mesh):

time: 36.3 us -> 31 us (0.85)
  local copies, waits for them, and re-layouts: 4.15 us -> 1.38 us
  Pallas kernels: 31.3 us -> 28.8 us
    unnamed x19 -> x1, local copies, waits for them, and re-layouts: 4.15 us -> 1.38 us
    pallas_call x1, Pallas kernels: 31.3 us -> 28.8 us  [on_device(): pl.pallas_call(functools.partial(kernel, bands, shards, side), out_shape=...]
where the time goes in v2:
time: 31 us; the launch traced here: 30.8 us
  Pallas kernels  28.8 us (93%)
  local copies, waits for them, and re-layouts  1.38 us (4%)
  between operations  0.66 us (2%)
    pallas_call x1, Pallas kernels, on_device(): pl.pallas_call(functools.partial(kernel, bands, shards, side), out_shape=...  28.8 us
    unnamed x1, local copies, waits for them, and re-layouts  1.38 us

profile of v2, /device:TPU:1, one launch (start us, length us, event | category | flops | bytes accessed | tf_op | source)
XLA Modules:
  0.0 30.8 jit_solution(7020358957801939143)
XLA Ops:
  0.7 28.8 %shard_map.91 = f32[4,1,16,128]{3,2,1,0:T(8,128)} custom-call(bf16[1,64,8192]{2,1,0:T(8,128)(2,1)} %tod.1, bf16[1,64,2049]{2,1,0:T(8,128)(2,1)} %taps_hbm.1, f32[1,64]{1,0:T(1,128)} %weights_hbm.1, s32[1,64]{1,0:T(1,128)} %bitcast.3, s32[1,64]{1,0:T(1,128)} %tile_row_hbm.1, s32[1,1]{1,0:T(1,128)S(6)} %copy.11.counts_hbm, f32[1,2,33]{2,1,0:T(2,128)} %beam_rows_hbm.1, ...), custom_call_target="tpu_custom_call" | custom-call | tf_op jit(solution)/shard_map/pallas_call | solution.py:465
  29.4 1.4 %copy.12 = f32[4,1,16,128]{3,2,1,0:T(8,128)} copy(f32[4,1,16,128]{3,2,1,0:T(8,128)} %shard_map.91) | data formatting | bytes 65536

commit v3 on v2

--- a/solution.py
+++ b/solution.py
@@ -16,8 +16,8 @@
 NBEAM = 2
 NCOMP = 4
 CHUNK = 1024
+PARTS = 4
 STEP = CHUNK // PIX
-ALL = (0, 1, 2, 3)
 MESH = pl.DeviceIdType.MESH
 F32 = jnp.float32
 BF16 = jnp.bfloat16
@@ -52,10 +52,10 @@
             [taps[0, :, pl.ds(pair * j + PIX * e, PIX)].astype(F32) * column for e in range(2)],
             axis=0,
         )
-        high, low = split(both)
+        turned = dot_nt(flip, jnp.concatenate(split(both), axis=0)).astype(BF16)
         lanes = pl.ds(2 * det * j, 2 * det)
-        table[0:PIX, lanes] = dot_nt(flip, high).astype(BF16)
-        table[PIX : 2 * PIX, lanes] = dot_nt(flip, low).astype(BF16)
+        table[0:PIX, lanes] = turned[:, 0 : 2 * det]
+        table[PIX : 2 * PIX, lanes] = turned[:, 2 * det :]
     last = taps[0, :, 2 * HALF : 2 * HALF + 1].astype(F32) * column
     last_high = last.astype(BF16).astype(F32)
     spot = iota((det, 2 * det), 1) == iota((det, 2 * det), 0) + det
@@ -69,20 +69,27 @@
     ).astype(BF16)
 
 
-def lagged_sums(x, table, block, parts):
+def lagged_sums(x, table, sums, block, blocks):
     det = x.shape[0]
-    total = None
-    for q in parts:
-        window = jnp.concatenate(
-            [
-                x[:, pl.ds(pl.multiple_of(PIX * block, PIX) + PIX * (4 * q + e), CHUNK)]
-                for e in range(4)
-            ],
-            axis=0,
-        )
-        part = dot(table[:, 4 * det * q : 4 * det * (q + 1)], window)
-        total = part if total is None else total + part
-    return total
+    top = 2 * PIX
+    for piece in range(2):
+        first = block + piece * STEP // 2
+        lanes = pl.ds(piece * CHUNK // 2, CHUNK // 2)
+        total = last = None
+        for q in (3, 2, 1, 0):
+            if first + STEP // 2 + 4 * q + 3 <= LAGS or first + 4 * q >= blocks + LAGS:
+                continue
+            window = jnp.concatenate(
+                [x[:, pl.ds(PIX * (first + 4 * q + e), CHUNK // 2)] for e in range(4)], axis=0
+            )
+            rows = top + 16 if q == 3 else top
+            part = dot(table[0:rows, 4 * det * q : 4 * det * (q + 1)], window)
+            if q == 3:
+                last = part[top:]
+            total = part[0:top] if total is None else total + part[0:top]
+        shape = (top, CHUNK // 2)
+        sums[0:top, lanes] = jnp.zeros(shape, F32) if total is None else total
+        sums[pl.ds(top, 16), lanes] = jnp.zeros((16, CHUNK // 2), F32) if last is None else last
 
 
 def add_diagonals(sums, here, before, block):
@@ -123,16 +130,15 @@
     weights_hbm,
     owner_hbm,
     tile_row_hbm,
-    counts_hbm,
     beam_rows_hbm,
     beam_cols_hbm,
     mixing_hbm,
+    counts,
     out,
     taps,
     weights,
     owner,
     tile_row,
-    counts,
     beam_rows,
     beam_cols,
     mixing,
@@ -187,7 +193,6 @@
         (
             (owner_hbm, owner),
             (tile_row_hbm, tile_row),
-            (counts_hbm, counts),
             (mixing_hbm, mixing),
             (weights_hbm, weights),
             (taps_hbm, taps),
@@ -197,8 +202,15 @@
     ):
         loads.append(pltpu.make_async_copy(source, target, small_sem.at[n]))
         loads[-1].start()
-    load = pltpu.make_async_copy(tod.at[0], x.at[:, pl.ds(2 * HALF, samples)], load_sem)
-    load.start()
+    loads_x = []
+    for n in range(PARTS):
+        rows = pl.ds(n * tod.shape[1] // PARTS, tod.shape[1] // PARTS)
+        loads_x.append(
+            pltpu.make_async_copy(
+                tod.at[0, rows], x.at[rows, pl.ds(2 * HALF, samples)], load_sem.at[n]
+            )
+        )
+        loads_x[-1].start()
 
     order = sorted(range(1, shards), key=lambda i: -hops(i))
 
@@ -222,10 +234,11 @@
     for start in (0, samples + 2 * HALF):
         x[:, pl.ds(start, 2 * HALF)] = jnp.zeros((x.shape[0], 2 * HALF), BF16)
 
+    for copy in loads:
+        copy.wait()
+
     row_i, lane_i = iota((blocks, blocks), 0), iota((blocks, blocks), 1)
     diagonal = row_i == lane_i
-    for copy in loads[:4]:
-        copy.wait()
     owner_row = owner[0:1, :]
     owner_col = jnp.sum(jnp.where(diagonal, owner_row, 0), axis=1, keepdims=True)
     same = (owner_col == owner_row) & (row_i < lane_i)
@@ -233,7 +246,7 @@
     ox, oz = owner_row // side, owner_row % side
     group = ((ox - sx + depth) % depth) * side + (oz - sz + side) % side
     slot_row = group * CAP + rank_row
-    kept = iota((1, blocks), 1) < counts[0:1, 0:1]
+    kept = iota((1, blocks), 1) < counts[0, 0]
     slots = shards * CAP
     pick = jnp.where((iota((slots, blocks), 0) == slot_row) & kept, 1.0, 0.0).astype(BF16)
     row_col = jnp.sum(jnp.where(diagonal, tile_row[0:1, :], 0), axis=1, keepdims=True)
@@ -247,24 +260,25 @@
     mix_out[...] = mix
     mix_in[0] = mix
 
-    for copy in loads[4:]:
+    lag_table(taps, weights, table)
+    for copy in loads_x:
         copy.wait()
-    lag_table(taps, weights, table)
-    load.wait()
-
-    even[...] = lagged_sums(x, table, blocks + STEP, (0, 1))
-    odd[...] = lagged_sums(x, table, 0, (2, 3))
+
+    def sums_of(target, block):
+        lagged_sums(x, table, target, block, blocks)
+
+    sums_of(even, blocks + STEP)
+    sums_of(odd, 0)
     add_diagonals(even, here, before, blocks + STEP)
 
-    def two_chunks(i, carry):
-        block = pl.multiple_of(STEP + 2 * STEP * i, STEP)
-        even[...] = lagged_sums(x, table, block, ALL)
-        add_diagonals(odd, here, before, pl.multiple_of(block - STEP, STEP))
-        odd[...] = lagged_sums(x, table, pl.multiple_of(block + STEP, STEP), ALL)
+    def two_chunks(block):
+        sums_of(even, block)
+        add_diagonals(odd, here, before, block - STEP)
+        sums_of(odd, block + STEP)
         add_diagonals(even, here, before, block)
-        return carry
-
-    lax.fori_loop(0, 2, two_chunks, 0)
+
+    for i in range(2):
+        two_chunks(STEP + 2 * STEP * i)
     overhang[0] = here[0:STEP, :] + before[pl.ds(1, STEP), :]
     overhang[1] = here[pl.ds(blocks + STEP, STEP), :] + before[pl.ds(blocks + STEP + 1, STEP), :]
 
@@ -329,7 +343,8 @@
             device_id_type=MESH,
         ).start()
 
-    lax.fori_loop(2, blocks // (2 * STEP), two_chunks, 0)
+    for i in range(2, blocks // (2 * STEP)):
+        two_chunks(STEP + 2 * STEP * i)
     add_diagonals(odd, here, before, blocks)
 
     for side_of, exists in enumerate((has_left, has_right)):
@@ -465,14 +480,14 @@
     return pl.pallas_call(
         functools.partial(kernel, bands, shards, side),
         out_shape=jax.ShapeDtypeStruct((NCOMP, 1, REACH, PIX), F32),
-        in_specs=[pl.BlockSpec(memory_space=pltpu.HBM)] * 9,
+        in_specs=[pl.BlockSpec(memory_space=pltpu.HBM)] * 8
+        + [pl.BlockSpec(memory_space=pltpu.SMEM)],
         out_specs=vmem,
         scratch_shapes=[
             pltpu.VMEM(filter_taps.shape, BF16),
             pltpu.VMEM((1, det), F32),
             pltpu.VMEM((1, blocks), jnp.int32),
             pltpu.VMEM((1, blocks), jnp.int32),
-            pltpu.VMEM((1, 1), jnp.int32),
             pltpu.VMEM(beam_rows.shape, F32),
             pltpu.VMEM(beam_cols.shape, F32),
             pltpu.VMEM((1, NBEAM, NCOMP), F32),
@@ -493,8 +508,8 @@
             pltpu.VMEM((NBEAM, long, PIX), F32),
             pltpu.VMEM((bands, NBEAM, REACH, PIX), F32),
             pltpu.VMEM((bands, NBEAM, REACH, PIX), F32),
-            pltpu.SemaphoreType.DMA,
-            pltpu.SemaphoreType.DMA((8,)),
+            pltpu.SemaphoreType.DMA((PARTS,)),
+            pltpu.SemaphoreType.DMA((7,)),
             pltpu.SemaphoreType.DMA((2,)),
             pltpu.SemaphoreType.DMA((2,)),
             pltpu.SemaphoreType.DMA((2,)),
@@ -505,18 +520,18 @@
             pltpu.SemaphoreType.DMA((bands,)),
         ],
         compiler_params=pltpu.CompilerParams(
-            collective_id=0, has_side_effects=True, vmem_limit_bytes=67043328
+            collective_id=0, has_side_effects=True, vmem_limit_bytes=50331648
         ),
     )(
-        tod,
+        *(pltpu.with_memory_space_constraint(v, pltpu.HBM) for v in (tod,
         filter_taps,
         det_weights,
         owner.reshape(1, blocks),
         tile_row,
-        block_counts,
         beam_rows,
         beam_cols,
-        mixing.transpose(1, 2, 0),
+        mixing.transpose(1, 2, 0),)),
+        block_counts,
     )
 
 

time: 31 us -> 28.1 us (0.906)
  Pallas kernels: 28.8 us -> 26.5 us
  local copies, waits for them, and re-layouts: 1.38 us -> 0.62 us
    pallas_call x1, Pallas kernels: 28.8 us -> 26.5 us  [on_device(): pl.pallas_call(functools.partial(kernel, bands, shards, side), out_shape=...]
    unnamed x1, local copies, waits for them, and re-layouts: 1.38 us -> 0.62 us
where the time goes in v3:
time: 28.1 us; the launch traced here: 27.8 us
  Pallas kernels  26.5 us (94%)
  between operations  0.66 us (2%)
  local copies, waits for them, and re-layouts  0.62 us (2%)
    pallas_call x1, Pallas kernels, on_device(): pl.pallas_call(functools.partial(kernel, bands, shards, side), out_shape=...  26.5 us
    unnamed x1, local copies, waits for them, and re-layouts  0.62 us

profile of v3, /device:TPU:1, one launch (start us, length us, event | category | flops | bytes accessed | tf_op | source)
XLA Modules:
  0.0 27.8 jit_solution(14351488496121896205)
XLA Ops:
  0.7 26.5 %shard_map.91 = f32[4,1,16,128]{3,2,1,0:T(8,128)S(1)} custom-call(bf16[1,64,8192]{2,1,0:T(8,128)(2,1)} %tod.1, bf16[1,64,2049]{2,1,0:T(8,128)(2,1)} %taps_hbm.1, f32[1,64]{1,0:T(1,128)} %weights_hbm.1, s32[1,64]{1,0:T(1,128)} %bitcast.3, s32[1,64]{1,0:T(1,128)} %tile_row_hbm.1, f32[1,2,33]{2,1,0:T(2,128)} %beam_rows_hbm.1, f32[1,2,33]{2,1,0:T(2,128)} %beam_cols_hbm.1, ...), custom_call_target="tpu_custom_call" | custom-call | tf_op jit(solution)/shard_map/pallas_call | solution.py:480
  27.1 0.6 %copy.12 = f32[4,1,16,128]{3,2,1,0:T(8,128)} copy(f32[4,1,16,128]{3,2,1,0:T(8,128)S(1)} %shard_map.91) | data formatting | bytes 65536

commit v4 on v3

--- a/solution.py
+++ b/solution.py
@@ -234,7 +234,7 @@
     for start in (0, samples + 2 * HALF):
         x[:, pl.ds(start, 2 * HALF)] = jnp.zeros((x.shape[0], 2 * HALF), BF16)
 
-    for copy in loads:
+    for copy in loads[:3]:
         copy.wait()
 
     row_i, lane_i = iota((blocks, blocks), 0), iota((blocks, blocks), 1)
@@ -250,16 +250,21 @@
     slots = shards * CAP
     pick = jnp.where((iota((slots, blocks), 0) == slot_row) & kept, 1.0, 0.0).astype(BF16)
     row_col = jnp.sum(jnp.where(diagonal, tile_row[0:1, :], 0), axis=1, keepdims=True)
-    row_hot = jnp.where(iota((blocks, PIX), 1) == row_col, 1.0, 0.0).astype(BF16)
-    meta = dot(pick, row_hot)
+    ahead = (owner_col == owner_row) & (lane_i < row_i)
+    rank_col = jnp.sum(jnp.where(ahead, 1, 0), axis=1, keepdims=True)
+    goes = jnp.where((iota((shards, blocks), 0) == group) & kept, 1.0, 0.0).astype(BF16)
+    rows_in = jnp.where(iota((blocks, PIX), 1) == rank_col, (row_col + 1).astype(F32), 0.0)
+    meta = dot(goes, rows_in.astype(BF16))
     meta_out[...] = meta
-    meta_in[0:CAP, :] = meta[0:CAP, :]
+    meta_in[0:1, :] = meta[0:1, :]
     mix = jnp.concatenate(
         [jnp.broadcast_to(mixing[0, :, c : c + 1], (NBEAM, PIX)) for c in range(NCOMP)], axis=0
     )
     mix_out[...] = mix
     mix_in[0] = mix
 
+    for copy in loads[3:]:
+        copy.wait()
     lag_table(taps, weights, table)
     for copy in loads_x:
         copy.wait()
@@ -317,22 +322,22 @@
     def _():
         to_left.start()
 
-    def to_shards(source, target, which):
+    def to_shards(source, target, rows, which):
         for i in order:
             pltpu.make_async_remote_copy(
-                source.at[pl.ds(CAP * i, CAP)],
-                target.at[pl.ds(CAP * i, CAP)],
+                source.at[pl.ds(rows * i, rows)],
+                target.at[pl.ds(rows * i, rows)],
                 peer_send.at[which],
                 peer_recv.at[which],
                 device_id=(band, shard_peer(i)),
                 device_id_type=MESH,
             ).start()
 
-    def from_shards(ref, sem):
-        part = ref.at[pl.ds(CAP, slots - CAP)]
+    def from_shards(ref, rows, sem):
+        part = ref.at[pl.ds(rows, rows * (shards - 1))]
         pltpu.make_async_copy(part, part, sem).wait()
 
-    to_shards(meta_out, meta_in, 0)
+    to_shards(meta_out, meta_in, 1, 0)
     for i in range(1, bands):
         pltpu.make_async_remote_copy(
             mix_out,
@@ -367,7 +372,7 @@
     values = dot(pick, value_high) + dot(pick, value_low)
     vals_out[...] = values
     vals_in[0:CAP, :] = values[0:CAP, :]
-    to_shards(vals_out, vals_in, 1)
+    to_shards(vals_out, vals_in, CAP, 1)
 
     long = span + 2 * REACH
     row_mats = jnp.concatenate(
@@ -375,21 +380,24 @@
         axis=0,
     )
     rows_high, rows_low = split(row_mats)
-    from_shards(meta_in, peer_recv.at[0])
-    hot = meta_in[...].astype(BF16)
+    from_shards(meta_in, 1, peer_recv.at[0])
+    slot_i, slot_lane = iota((slots, PIX), 0), iota((slots, PIX), 1)
+    spread = jnp.where(iota((slots, shards), 0) // CAP == iota((slots, shards), 1), 1.0, 0.0)
+    listed = dot(spread.astype(BF16), meta_in[...].astype(BF16))
+    row_of = jnp.sum(jnp.where(slot_i % CAP == slot_lane, listed, 0.0), axis=1, keepdims=True)
+    hot = jnp.where((slot_lane + 1).astype(F32) == row_of, 1.0, 0.0).astype(BF16)
     slot_high = dot_nt(rows_high, hot).astype(BF16)
     slot_low = dot_nt(rows_low, hot).astype(BF16)
     cols = [split(band_rows(beam_cols[0, k : k + 1, :], PIX, REACH)) for k in range(NBEAM)]
 
-    from_shards(vals_in, peer_recv.at[1])
+    from_shards(vals_in, CAP, peer_recv.at[1])
     in_high, in_low = split(vals_in[...])
-    rowed = dot(slot_high, in_high) + dot(slot_high, in_low) + dot(slot_low, in_high)
+    both = dot(slot_high, jnp.concatenate([in_high, in_low], axis=1))
+    rowed = both[:, 0:PIX] + both[:, PIX:] + dot(slot_low, in_high)
     for k in range(NBEAM):
         rowed_high, rowed_low = split(rowed[long * k : long * (k + 1), :])
-        col_high, col_low = cols[k]
-        wide[k] = (
-            dot_nt(rowed_high, col_high) + dot_nt(rowed_low, col_high) + dot_nt(rowed_high, col_low)
-        )
+        both = dot_nt(rowed_high, jnp.concatenate(cols[k], axis=0))
+        wide[k] = both[:, 0:PIX] + both[:, PIX:] + dot_nt(rowed_low, cols[k][0])
 
     below = pltpu.make_async_remote_copy(
         wide.at[:, pl.ds(REACH + span, REACH), :],
@@ -459,8 +467,8 @@
         to_left.wait_send()
         above.wait_send()
 
-    from_shards(meta_out, peer_send.at[0])
-    from_shards(vals_out, peer_send.at[1])
+    from_shards(meta_out, 1, peer_send.at[0])
+    from_shards(vals_out, CAP, peer_send.at[1])
     for i in range(1, bands):
         pltpu.make_async_copy(mix_out, mix_out, band_send.at[0, i]).wait()
     for copy in sends:
@@ -499,8 +507,8 @@
             pltpu.VMEM((2 * PIX + 16, CHUNK), F32),
             pltpu.VMEM((2, STEP, PIX), F32),
             pltpu.VMEM((2, STEP, PIX), F32),
-            pltpu.VMEM((slots, PIX), F32),
-            pltpu.VMEM((slots, PIX), F32),
+            pltpu.VMEM((shards, PIX), F32),
+            pltpu.VMEM((shards, PIX), F32),
             pltpu.VMEM((slots, PIX), F32),
             pltpu.VMEM((slots, PIX), F32),
             pltpu.VMEM((NCOMP * NBEAM, PIX), F32),

time: 28.1 us -> 27.7 us (0.986)
  no operation moved by 1% of the time
where the time goes in v4:
time: 27.7 us; the launch traced here: 27.6 us
  Pallas kernels  26.3 us (95%)
  between operations  0.66 us (2%)
  local copies, waits for them, and re-layouts  0.62 us (2%)
    pallas_call x1, Pallas kernels, on_device(): pl.pallas_call(functools.partial(kernel, bands, shards, side), out_shape=...  26.3 us
    unnamed x1, local copies, waits for them, and re-layouts  0.62 us

profile of v4, /device:TPU:1, one launch (start us, length us, event | category | flops | bytes accessed | tf_op | source)
XLA Modules:
  0.0 27.6 jit_solution(4514829859953821044)
XLA Ops:
  0.7 26.3 %shard_map.91 = f32[4,1,16,128]{3,2,1,0:T(8,128)S(1)} custom-call(bf16[1,64,8192]{2,1,0:T(8,128)(2,1)} %tod.1, bf16[1,64,2049]{2,1,0:T(8,128)(2,1)} %taps_hbm.1, f32[1,64]{1,0:T(1,128)} %weights_hbm.1, s32[1,64]{1,0:T(1,128)} %bitcast.3, s32[1,64]{1,0:T(1,128)} %tile_row_hbm.1, f32[1,2,33]{2,1,0:T(2,128)} %beam_rows_hbm.1, f32[1,2,33]{2,1,0:T(2,128)} %beam_cols_hbm.1, ...), custom_call_target="tpu_custom_call" | custom-call | tf_op jit(solution)/shard_map/pallas_call | solution.py:488
  27.0 0.6 %copy.12 = f32[4,1,16,128]{3,2,1,0:T(8,128)} copy(f32[4,1,16,128]{3,2,1,0:T(8,128)S(1)} %shard_map.91) | data formatting | bytes 65536

commit v5 on v4

--- a/solution.py
+++ b/solution.py
@@ -191,11 +191,11 @@
     loads = []
     for n, (source, target) in enumerate(
         (
+            (taps_hbm, taps),
+            (weights_hbm, weights),
             (owner_hbm, owner),
             (tile_row_hbm, tile_row),
             (mixing_hbm, mixing),
-            (weights_hbm, weights),
-            (taps_hbm, taps),
             (beam_rows_hbm, beam_rows),
             (beam_cols_hbm, beam_cols),
         )
@@ -234,7 +234,10 @@
     for start in (0, samples + 2 * HALF):
         x[:, pl.ds(start, 2 * HALF)] = jnp.zeros((x.shape[0], 2 * HALF), BF16)
 
-    for copy in loads[:3]:
+    for copy in loads[:2]:
+        copy.wait()
+    lag_table(taps, weights, table)
+    for copy in loads[2:] + loads_x:
         copy.wait()
 
     row_i, lane_i = iota((blocks, blocks), 0), iota((blocks, blocks), 1)
@@ -263,12 +266,6 @@
     mix_out[...] = mix
     mix_in[0] = mix
 
-    for copy in loads[3:]:
-        copy.wait()
-    lag_table(taps, weights, table)
-    for copy in loads_x:
-        copy.wait()
-
     def sums_of(target, block):
         lagged_sums(x, table, target, block, blocks)
 
@@ -369,7 +366,8 @@
         axis=0,
     )
     value_high, value_low = split(block_values)
-    values = dot(pick, value_high) + dot(pick, value_low)
+    both = dot(pick, jnp.concatenate([value_high, value_low], axis=1))
+    values = both[:, 0:PIX] + both[:, PIX:]
     vals_out[...] = values
     vals_in[0:CAP, :] = values[0:CAP, :]
     to_shards(vals_out, vals_in, CAP, 1)
@@ -425,7 +423,7 @@
         above.start()
 
     sends = []
-    for i in range(1, bands):
+    for i in sorted(range(1, bands), key=lambda i: -min(i, bands - i)):
         peer = lax.rem(band + i, bands)
         copy = pltpu.make_async_remote_copy(
             wide.at[:, pl.ds(pl.multiple_of(REACH + share * peer, REACH), share), :],

time: 27.7 us -> 27.4 us (0.989)
  Pallas kernels: 26.3 us -> 26 us
    pallas_call x1, Pallas kernels: 26.3 us -> 26 us  [on_device(): pl.pallas_call(functools.partial(kernel, bands, shards, side), out_shape=...]
where the time goes in v5:
time: 27.4 us; the launch traced here: 27.3 us
  Pallas kernels  26 us (95%)
  between operations  0.66 us (2%)
  local copies, waits for them, and re-layouts  0.62 us (2%)
    pallas_call x1, Pallas kernels, on_device(): pl.pallas_call(functools.partial(kernel, bands, shards, side), out_shape=...  26 us
    unnamed x1, local copies, waits for them, and re-layouts  0.62 us

profile of v5, /device:TPU:1, one launch (start us, length us, event | category | flops | bytes accessed | tf_op | source)
XLA Modules:
  0.0 27.3 jit_solution(7864543591864495145)
XLA Ops:
  0.7 26.0 %shard_map.91 = f32[4,1,16,128]{3,2,1,0:T(8,128)S(1)} custom-call(bf16[1,64,8192]{2,1,0:T(8,128)(2,1)} %tod.1, bf16[1,64,2049]{2,1,0:T(8,128)(2,1)} %taps_hbm.1, f32[1,64]{1,0:T(1,128)} %weights_hbm.1, s32[1,64]{1,0:T(1,128)} %bitcast.3, s32[1,64]{1,0:T(1,128)} %tile_row_hbm.1, f32[1,2,33]{2,1,0:T(2,128)} %beam_rows_hbm.1, f32[1,2,33]{2,1,0:T(2,128)} %beam_cols_hbm.1, ...), custom_call_target="tpu_custom_call" | custom-call | tf_op jit(solution)/shard_map/pallas_call | solution.py:486
  26.6 0.6 %copy.12 = f32[4,1,16,128]{3,2,1,0:T(8,128)} copy(f32[4,1,16,128]{3,2,1,0:T(8,128)S(1)} %shard_map.91) | data formatting | bytes 65536

commit v6 on v5

--- a/solution.py
+++ b/solution.py
@@ -319,8 +319,8 @@
     def _():
         to_left.start()
 
-    def to_shards(source, target, rows, which):
-        for i in order:
+    def to_shards(source, target, rows, which, peers):
+        for i in peers:
             pltpu.make_async_remote_copy(
                 source.at[pl.ds(rows * i, rows)],
                 target.at[pl.ds(rows * i, rows)],
@@ -334,7 +334,7 @@
         part = ref.at[pl.ds(rows, rows * (shards - 1))]
         pltpu.make_async_copy(part, part, sem).wait()
 
-    to_shards(meta_out, meta_in, 1, 0)
+    to_shards(meta_out, meta_in, 1, 0, order)
     for i in range(1, bands):
         pltpu.make_async_remote_copy(
             mix_out,
@@ -366,11 +366,21 @@
         axis=0,
     )
     value_high, value_low = split(block_values)
-    both = dot(pick, jnp.concatenate([value_high, value_low], axis=1))
-    values = both[:, 0:PIX] + both[:, PIX:]
-    vals_out[...] = values
-    vals_in[0:CAP, :] = values[0:CAP, :]
-    to_shards(vals_out, vals_in, CAP, 1)
+    packed = jnp.concatenate([value_high, value_low], axis=1)
+
+    def fill(first, count):
+        both = dot(pick[first : first + count], packed)
+        values = both[:, 0:PIX] + both[:, PIX:]
+        vals_out[pl.ds(first, count), :] = values
+        return values
+
+    quarter = slots // 4
+    early = [i for i in order if quarter <= i * CAP < 3 * quarter and hops(i) >= 4]
+    fill(quarter, 2 * quarter)
+    to_shards(vals_out, vals_in, CAP, 1, early)
+    vals_in[0:CAP, :] = fill(0, quarter)[0:CAP, :]
+    fill(3 * quarter, quarter)
+    to_shards(vals_out, vals_in, CAP, 1, [i for i in order if i not in early])
 
     long = span + 2 * REACH
     row_mats = jnp.concatenate(

time: 27.4 us -> 27.4 us (level)
  no operation moved by 1% of the time
where the time goes in v6:
time: 27.4 us; the launch traced here: 27.2 us
  Pallas kernels  25.9 us (95%)
  between operations  0.66 us (2%)
  local copies, waits for them, and re-layouts  0.62 us (2%)
    pallas_call x1, Pallas kernels, on_device(): pl.pallas_call(functools.partial(kernel, bands, shards, side), out_shape=...  25.9 us
    unnamed x1, local copies, waits for them, and re-layouts  0.62 us

profile of v6, /device:TPU:1, one launch (start us, length us, event | category | flops | bytes accessed | tf_op | source)
XLA Modules:
  0.0 27.2 jit_solution(1421363459656148182)
XLA Ops:
  0.7 25.9 %shard_map.91 = f32[4,1,16,128]{3,2,1,0:T(8,128)S(1)} custom-call(bf16[1,64,8192]{2,1,0:T(8,128)(2,1)} %tod.1, bf16[1,64,2049]{2,1,0:T(8,128)(2,1)} %taps_hbm.1, f32[1,64]{1,0:T(1,128)} %weights_hbm.1, s32[1,64]{1,0:T(1,128)} %bitcast.3, s32[1,64]{1,0:T(1,128)} %tile_row_hbm.1, f32[1,2,33]{2,1,0:T(2,128)} %beam_rows_hbm.1, f32[1,2,33]{2,1,0:T(2,128)} %beam_cols_hbm.1, ...), custom_call_target="tpu_custom_call" | custom-call | tf_op jit(solution)/shard_map/pallas_call | solution.py:496
  26.6 0.6 %copy.12 = f32[4,1,16,128]{3,2,1,0:T(8,128)} copy(f32[4,1,16,128]{3,2,1,0:T(8,128)S(1)} %shard_map.91) | data formatting | bytes 65536
